TPU v7x, 32 devices: a whole 2x2x4 slice. The times are simulated.
32 devices in a mesh: wide: 8 (over z, y), narrow: 4 (over x, core).
Axes of the slice: x: 2, y: 2, z: 4, core: 2. Of those that a mesh axis runs over, the one named last changes fastest.
Arguments:
- media_feats: bfloat16 [8, 2048, 1536], P('wide', 'narrow'), may hold values from -6 to 6
- latents: bfloat16 [8, 64, 1536], P('wide', 'narrow'), may hold values from -6 to 6
- frame_counts: int32 [8], P('wide'), may hold values from 1 to 8, as said below
- media_mask: int32 [8, 2048], P('wide'), may hold values 0 or 1
- time_embed: bfloat16 [8, 1536], replicated, may hold values from -3 to 3
- media_gain: float32 [1536], replicated, may hold values from 0.1 to 1.9
- media_bias: float32 [1536], replicated, may hold values from -1.75 to 1.75
- latent_gain: float32 [1536], replicated, may hold values from 0.1 to 1.9
- latent_bias: float32 [1536], replicated, may hold values from -1.75 to 1.75
- ffn_gain: float32 [1536], replicated, may hold values from 0.1 to 1.9
- ffn_bias: float32 [1536], replicated, may hold values from -1.75 to 1.75
- query_weight: bfloat16 [1536, 1536], P('wide', 'narrow'), may hold values from -0.3125 to 0.3125
- keyval_weight: bfloat16 [1536, 2, 1536], P('wide', None, 'narrow'), may hold values from -0.15625 to 0.15625
- output_weight: bfloat16 [1536, 1536], P('narrow', 'wide'), may hold values from -0.625 to 0.625
- up_weight: bfloat16 [1536, 6144], P(None, 'narrow'), may hold values from -0.15625 to 0.15625
- down_weight: bfloat16 [6144, 1536], P('narrow'), may hold values from -0.078125 to 0.078125
- cotangent: bfloat16 [8, 64, 1536], P('wide', 'narrow'), may hold values from -6 to 6
Outputs:
- out_latents: bfloat16 [8, 64, 1536], P('wide', 'narrow')
- grad_media: bfloat16 [8, 2048, 1536], P('wide', 'narrow')
- grad_latents: bfloat16 [8, 64, 1536], P('wide', 'narrow')
- grad_time_embed: float32 [8, 1536], P(None, ('wide', 'narrow'))
- grad_media_gain: float32 [1536], P(('wide', 'narrow'))
- grad_media_bias: float32 [1536], P(('wide', 'narrow'))
- grad_latent_gain: float32 [1536], P(('wide', 'narrow'))
- grad_latent_bias: float32 [1536], P(('wide', 'narrow'))
- grad_ffn_gain: float32 [1536], P(('wide', 'narrow'))
- grad_ffn_bias: float32 [1536], P(('wide', 'narrow'))
- grad_query_weight: float32 [1536, 1536], P('wide', 'narrow')
- grad_keyval_weight: float32 [1536, 2, 1536], P('wide', None, 'narrow')
- grad_output_weight: float32 [1536, 1536], P('narrow', 'wide')
- grad_up_weight: float32 [1536, 6144], P('wide', 'narrow')
- grad_down_weight: float32 [6144, 1536], P('narrow', 'wide')
Inputs may be any that keep to these rules, and one draw needn't show every extreme that they name: `frame_counts`: frames of each item; some item has exactly 8.
All inputs are finite; a program needn't handle non-finite values. No bound on the sum of `media_mask` on one device may be relied on, other than what follows from the above.
Results may differ from a plain program's by a relative error of at most 0.02.
Values may be sent and summed in bfloat16 or wider, within the bound.
A program may use at most 128 MiB of HBM per device.

v0:
```python
import math
import jax
import jax.numpy as jnp
from jax import lax
from jax.sharding import PartitionSpec as P

HEADS = 16
HEAD_DIM = 96
FRAMES_MAX = 8
PATCHES = 256
EPS = 1e-05
ENT_COEF = 4.0
HIGH = lax.Precision.HIGHEST


def norm_forward(values, norm_gain, norm_bias):
    row_mean = jnp.mean(values, axis=-1, keepdims=True)
    centered = values - row_mean
    inv_std = lax.rsqrt(jnp.mean(centered * centered, axis=-1, keepdims=True) + EPS)
    normed = centered * inv_std
    return (normed * norm_gain + norm_bias, normed, inv_std)


def norm_backward(grad_out, normed, inv_std, norm_gain):
    scaled = grad_out * norm_gain
    grad_in = inv_std * (
        scaled
        - jnp.mean(scaled, axis=-1, keepdims=True)
        - normed * jnp.mean(scaled * normed, axis=-1, keepdims=True)
    )
    return (grad_in, jnp.sum(grad_out * normed, axis=0), jnp.sum(grad_out, axis=0))


def gelu_slope(pre_act):
    cdf_part = 0.5 * (1.0 + lax.erf(pre_act * (1.0 / math.sqrt(2.0))))
    density = jnp.exp(-0.5 * pre_act * pre_act) * (1.0 / math.sqrt(2.0 * math.pi))
    return cdf_part + pre_act * density


def body(
    media_feats,
    latents,
    frame_counts,
    media_mask,
    time_embed,
    media_gain,
    media_bias,
    latent_gain,
    latent_bias,
    ffn_gain,
    ffn_bias,
    query_weight,
    keyval_weight,
    output_weight,
    up_weight,
    down_weight,
    cotangent,
):
    item_count = media_feats.shape[0]
    own_media = media_feats.shape[1]
    width = media_feats.shape[2]
    own_latent = latents.shape[1]
    narrow_size = lax.axis_size("narrow")
    narrow_pos = lax.axis_index("narrow")
    media_total = own_media * narrow_size
    latent_total = own_latent * narrow_size
    head_local = HEADS // narrow_size
    cols = head_local * HEAD_DIM
    key_total = media_total + latent_total
    all_ids = jnp.arange(media_total, dtype=jnp.int32) // PATCHES
    valid_tok = (all_ids[None, :] < frame_counts[:, None]) & (media_mask > 0)
    local_count = jnp.sum(valid_tok.astype(jnp.float32)) + float(item_count * latent_total)
    total_count = lax.psum(local_count, "wide")
    all_items = item_count * lax.axis_size("wide")
    ent_weight = ENT_COEF * float(all_items * media_total) / total_count
    query_own, keyval_own, output_own = (
        lax.all_gather(query_weight, "wide", axis=0, tiled=True),
        lax.all_gather(keyval_weight, "wide", axis=0, tiled=True),
        lax.all_gather(output_weight, "wide", axis=1, tiled=True),
    )
    query_full, keyval_full = (
        lax.all_gather(query_own, "narrow", axis=1, tiled=True),
        lax.all_gather(keyval_own, "narrow", axis=2, tiled=True),
    )
    keyval_flat = keyval_own.reshape(width, 2 * cols)
    own_ids = (narrow_pos * own_media + jnp.arange(own_media, dtype=jnp.int32)) // PATCHES
    frame_onehot = own_ids[:, None] == jnp.arange(FRAMES_MAX, dtype=jnp.int32)[None, :]
    time_rows = jnp.dot(
        frame_onehot.astype(jnp.bfloat16), time_embed, preferred_element_type=jnp.float32
    )
    score_scale = HEAD_DIM ** (-0.5)

    def item_step(carry, item):
        (
            down_acc,
            up_acc,
            output_acc,
            keyval_acc,
            query_acc,
            mg_acc,
            mb_acc,
            lg_acc,
            lb_acc,
            fg_acc,
            fb_acc,
            time_acc,
        ) = carry
        media_one, latent_one, valid_one, cot_one = item
        media_nf, media_hat, media_istd = norm_forward(
            media_one.astype(jnp.float32) + time_rows, media_gain, media_bias
        )
        latent_f32 = latent_one.astype(jnp.float32)
        latent_nf, latent_hat, latent_istd = norm_forward(latent_f32, latent_gain, latent_bias)
        media_all, latent_all = (
            lax.all_gather(media_nf.astype(jnp.bfloat16), "narrow", axis=0, tiled=True),
            lax.all_gather(latent_nf.astype(jnp.bfloat16), "narrow", axis=0, tiled=True),
        )
        keys_in = jnp.concatenate([media_all, latent_all], axis=0)
        query_act = jnp.dot(latent_all, query_own, preferred_element_type=jnp.float32).astype(
            jnp.bfloat16
        )
        key_vals = jnp.dot(keys_in, keyval_flat, preferred_element_type=jnp.float32).astype(
            jnp.bfloat16
        )
        query_heads = query_act.reshape(latent_total, head_local, HEAD_DIM)
        key_heads = key_vals[:, :cols].reshape(key_total, head_local, HEAD_DIM)
        value_heads = key_vals[:, cols:].reshape(key_total, head_local, HEAD_DIM)
        key_valid = jnp.concatenate([valid_one, jnp.ones((latent_total,), dtype=bool)])
        scores = (
            jnp.einsum("lhd,khd->hlk", query_heads, key_heads, preferred_element_type=jnp.float32)
            * score_scale
        )
        open_keys = key_valid[None, None, :]
        masked = jnp.where(open_keys, scores, -1e30)
        row_top = jnp.max(masked, axis=-1)
        expo = jnp.exp(masked - row_top[..., None])
        prob_all = expo / jnp.sum(expo, axis=-1)[..., None]
        prob_low = prob_all.astype(jnp.bfloat16)
        plain_scores = jnp.where(open_keys, scores, 0.0)
        mean_score = jnp.sum(prob_all * plain_scores, axis=-1)
        attn_out = jnp.einsum(
            "hlk,khd->lhd", prob_low, value_heads, preferred_element_type=jnp.float32
        ).reshape(latent_total, cols)
        attn_low = attn_out.astype(jnp.bfloat16)
        branch_part = jnp.dot(attn_low, output_own, preferred_element_type=jnp.float32)
        branch_own = lax.psum_scatter(
            branch_part.astype(jnp.bfloat16), "narrow", scatter_dimension=0, tiled=True
        ).astype(jnp.float32)
        latent_mid = latent_f32 + branch_own
        hidden_f, hidden_hat, hidden_istd = norm_forward(latent_mid, ffn_gain, ffn_bias)
        hidden_all, cot_all = (
            lax.all_gather(hidden_f.astype(jnp.bfloat16), "narrow", axis=0, tiled=True),
            lax.all_gather(cot_one, "narrow", axis=0, tiled=True),
        )
        pre_act = jnp.dot(hidden_all, up_weight, preferred_element_type=jnp.float32)
        act_low = jax.nn.gelu(pre_act, approximate=False).astype(jnp.bfloat16)
        ffn_part = jnp.dot(act_low, down_weight, preferred_element_type=jnp.float32)
        ffn_own = lax.psum_scatter(
            ffn_part.astype(jnp.bfloat16), "narrow", scatter_dimension=0, tiled=True
        ).astype(jnp.float32)
        out_one = (latent_mid + ffn_own).astype(jnp.bfloat16)
        down_acc = down_acc + jnp.einsum(
            "lf,ld->fd", act_low, cot_all, preferred_element_type=jnp.float32
        )
        grad_act = jnp.einsum("ld,fd->lf", cot_all, down_weight, preferred_element_type=jnp.float32)
        grad_pre = (grad_act * gelu_slope(pre_act)).astype(jnp.bfloat16)
        up_acc = up_acc + jnp.einsum(
            "ld,lf->df", hidden_all, grad_pre, preferred_element_type=jnp.float32
        )
        hidden_part = jnp.einsum(
            "lf,df->ld", grad_pre, up_weight, preferred_element_type=jnp.float32
        )
        grad_hidden = lax.psum_scatter(
            hidden_part.astype(jnp.bfloat16), "narrow", scatter_dimension=0, tiled=True
        ).astype(jnp.float32)
        grad_norm, fg_part, fb_part = norm_backward(grad_hidden, hidden_hat, hidden_istd, ffn_gain)
        grad_mid = cot_one.astype(jnp.float32) + grad_norm
        grad_branch_all = lax.all_gather(
            grad_mid.astype(jnp.bfloat16), "narrow", axis=0, tiled=True
        )
        output_acc = output_acc + jnp.einsum(
            "lc,ld->cd", attn_low, grad_branch_all, preferred_element_type=jnp.float32
        )
        grad_attn = jnp.einsum(
            "ld,cd->lc", grad_branch_all, output_own, preferred_element_type=jnp.float32
        ).astype(jnp.bfloat16)
        row_dots = jnp.sum(
            (grad_attn.astype(jnp.float32) * attn_out).reshape(latent_total, head_local, HEAD_DIM),
            axis=-1,
        )
        shift_rows = (jnp.transpose(row_dots, (1, 0)) - ent_weight * mean_score)[..., None]
        grad_heads = grad_attn.reshape(latent_total, head_local, HEAD_DIM)
        grad_prob = jnp.einsum(
            "lhd,khd->hlk", grad_heads, value_heads, preferred_element_type=jnp.float32
        )
        grad_scores = (prob_all * (grad_prob - ent_weight * plain_scores - shift_rows)).astype(
            jnp.bfloat16
        )
        grad_values = jnp.einsum(
            "hlk,lhd->khd", prob_low, grad_heads, preferred_element_type=jnp.float32
        ).reshape(key_total, cols)
        grad_keys = (
            jnp.einsum(
                "hlk,lhd->khd", grad_scores, query_heads, preferred_element_type=jnp.float32
            ).reshape(key_total, cols)
            * score_scale
        )
        grad_query = (
            jnp.einsum(
                "hlk,khd->lhd", grad_scores, key_heads, preferred_element_type=jnp.float32
            ).reshape(latent_total, cols)
            * score_scale
        ).astype(jnp.bfloat16)
        grad_pairs = jnp.concatenate([grad_keys, grad_values], axis=-1).astype(jnp.bfloat16)
        keyval_acc = keyval_acc + jnp.einsum(
            "kd,ke->de", keys_in, grad_pairs, preferred_element_type=jnp.float32
        )
        query_acc = query_acc + jnp.einsum(
            "ld,lc->dc", latent_all, grad_query, preferred_element_type=jnp.float32
        )
        media_pairs = grad_pairs[:media_total].reshape(media_total, 2, cols)
        latent_pairs = jnp.concatenate(
            [
                grad_pairs[media_total:].reshape(latent_total, 2, cols),
                grad_query.reshape(latent_total, 1, cols),
            ],
            axis=1,
        )
        media_back, latent_back = (
            lax.all_to_all(media_pairs, "narrow", split_axis=0, concat_axis=2, tiled=True),
            lax.all_to_all(latent_pairs, "narrow", split_axis=0, concat_axis=2, tiled=True),
        )
        grad_media_rows = jnp.einsum(
            "rsc,dsc->rd", media_back, keyval_full, preferred_element_type=jnp.float32
        )
        grad_latent_normed = jnp.einsum(
            "rsc,dsc->rd", latent_back[:, :2], keyval_full, preferred_element_type=jnp.float32
        ) + jnp.einsum(
            "rc,dc->rd", latent_back[:, 2], query_full, preferred_element_type=jnp.float32
        )
        grad_media_in, mg_part, mb_part = norm_backward(
            grad_media_rows, media_hat, media_istd, media_gain
        )
        time_acc = time_acc + jnp.einsum(
            "mf,md->fd", frame_onehot.astype(jnp.float32), grad_media_in, precision=HIGH
        )
        grad_latent_in, lg_part, lb_part = norm_backward(
            grad_latent_normed, latent_hat, latent_istd, latent_gain
        )
        grad_latent_one = (grad_mid + grad_latent_in).astype(jnp.bfloat16)
        carry = (
            down_acc,
            up_acc,
            output_acc,
            keyval_acc,
            query_acc,
            mg_acc + mg_part,
            mb_acc + mb_part,
            lg_acc + lg_part,
            lb_acc + lb_part,
            fg_acc + fg_part,
            fb_acc + fb_part,
            time_acc,
        )
        return (carry, (out_one, grad_media_in.astype(jnp.bfloat16), grad_latent_one))

    ff_local = up_weight.shape[1]
    vector_zero = jnp.zeros((width,), jnp.float32)
    start = (
        jnp.zeros((ff_local, width), jnp.float32),
        jnp.zeros((width, ff_local), jnp.float32),
        jnp.zeros((cols, width), jnp.float32),
        jnp.zeros((width, 2 * cols), jnp.float32),
        jnp.zeros((width, cols), jnp.float32),
        vector_zero,
        vector_zero,
        vector_zero,
        vector_zero,
        vector_zero,
        vector_zero,
        jnp.zeros((FRAMES_MAX, width), jnp.float32),
    )
    totals, stacked = lax.scan(item_step, start, (media_feats, latents, valid_tok, cotangent))
    (
        down_acc,
        up_acc,
        output_acc,
        keyval_acc,
        query_acc,
        mg_acc,
        mb_acc,
        lg_acc,
        lb_acc,
        fg_acc,
        fb_acc,
        time_acc,
    ) = totals
    out_latents, grad_media, grad_latents = stacked
    up_sum, down_sum, query_sum, keyval_sum, output_sum = (
        lax.psum_scatter(
            up_acc.astype(jnp.bfloat16), "wide", scatter_dimension=0, tiled=True
        ).astype(jnp.float32),
        lax.psum_scatter(
            down_acc.astype(jnp.bfloat16), "wide", scatter_dimension=1, tiled=True
        ).astype(jnp.float32),
        lax.psum_scatter(
            query_acc.astype(jnp.bfloat16), "wide", scatter_dimension=0, tiled=True
        ).astype(jnp.float32),
        lax.psum_scatter(
            keyval_acc.reshape(width, 2, cols).astype(jnp.bfloat16),
            "wide",
            scatter_dimension=0,
            tiled=True,
        ).astype(jnp.float32),
        lax.psum_scatter(
            output_acc.astype(jnp.bfloat16), "wide", scatter_dimension=1, tiled=True
        ).astype(jnp.float32),
    )
    mg_sum, mb_sum, lg_sum, lb_sum, fg_sum, fb_sum, time_sum = (
        lax.psum_scatter(mg_acc, ("wide", "narrow"), scatter_dimension=0, tiled=True),
        lax.psum_scatter(mb_acc, ("wide", "narrow"), scatter_dimension=0, tiled=True),
        lax.psum_scatter(lg_acc, ("wide", "narrow"), scatter_dimension=0, tiled=True),
        lax.psum_scatter(lb_acc, ("wide", "narrow"), scatter_dimension=0, tiled=True),
        lax.psum_scatter(fg_acc, ("wide", "narrow"), scatter_dimension=0, tiled=True),
        lax.psum_scatter(fb_acc, ("wide", "narrow"), scatter_dimension=0, tiled=True),
        lax.psum_scatter(time_acc, ("wide", "narrow"), scatter_dimension=1, tiled=True),
    )
    return (
        out_latents,
        grad_media,
        grad_latents,
        time_sum,
        mg_sum,
        mb_sum,
        lg_sum,
        lb_sum,
        fg_sum,
        fb_sum,
        query_sum,
        keyval_sum,
        output_sum,
        up_sum,
        down_sum,
    )


def solution(mesh):
    placed = (
        P("wide", "narrow", None),
        P("wide", "narrow", None),
        P("wide"),
        P("wide", None),
        P(),
        P(),
        P(),
        P(),
        P(),
        P(),
        P(),
        P("wide", "narrow"),
        P("wide", None, "narrow"),
        P("narrow", "wide"),
        P(None, "narrow"),
        P("narrow", None),
        P("wide", "narrow", None),
    )
    return jax.shard_map(
        body,
        mesh=mesh,
        in_specs=placed,
        out_specs=(
            P("wide", "narrow", None),
            P("wide", "narrow", None),
            P("wide", "narrow", None),
            P(None, ("wide", "narrow")),
            P(("wide", "narrow")),
            P(("wide", "narrow")),
            P(("wide", "narrow")),
            P(("wide", "narrow")),
            P(("wide", "narrow")),
            P(("wide", "narrow")),
            P("wide", "narrow"),
            P("wide", None, "narrow"),
            P("narrow", "wide"),
            P("wide", "narrow"),
            P("narrow", "wide"),
        ),
        check_vma=False,
    )
```

profile of v0, /device:TPU:0, one launch (start us, length us, event | category | flops | bytes accessed | tf_op | source)
XLA Modules:
  0.0 941.4 jit_solution(12498868731809088327)
XLA Ops:
  15.3 6.9 all_gather.36
  23.6 30.5 %all-gather.12.cloned.1.call-done = bf16[1536,384]{1,0:T(8,128)(2,1)} async-done(((bf16[192,384]{1,0:T(8,128)(2,1)}), bf16[1536,384]{1,0:T(8,128)(2,1)}) %all-gather.12.cloned.1.call-update) | async-done | bytes 1179664 | tf_op jit(solution)/shard_map/all_gather | solution.py:77
  55.8 51.6 %all-gather.10.cloned.1.call-done = bf16[1536,2,384]{2,0,1:T(8,128)(2,1)} async-done(((bf16[192,2,384]{2,0,1:T(8,128)(2,1)}), bf16[1536,2,384]{2,0,1:T(8,128)(2,1)}) %all-gather.10.cloned.1.call-update) | async-done | bytes 2359312 | tf_op jit(solution)/shard_map/all_gather | solution.py:78
  107.4 4.3 copy.117
  111.7 42.8 %all-gather.8.cloned.1.call-done = bf16[2048,1536]{1,0:T(8,128)(2,1)} async-done(((bf16[512,1536]{1,0:T(8,128)(2,1)}), bf16[2048,1536]{1,0:T(8,128)(2,1)}) %all-gather.8.cloned.1.call-update) | async-done | bytes 6291472 | tf_op jit(solution)/shard_map/while/body/eval_jaxpr/all_gather | solution.py:115
  154.4 3.3 constant_dynamic-update-slice_fusion.1
  157.9 5.5 convolution_convert_fusion.2
  165.4 3.7 copy.119
  169.2 3.8 copy.118
  173.0 3.6 fusion.82
  176.6 3.0 convolution_bitcast_fusion.3
  181.3 16.3 %all-gather.14.cloned.1.call-done = bf16[384,1536]{0,1:T(8,128)(2,1)} async-done(((bf16[384,192]{0,1:T(8,128)(2,1)}), bf16[384,1536]{0,1:T(8,128)(2,1)}) %all-gather.14.cloned.1.call-update) | async-done | bytes 1179664 | tf_op jit(solution)/shard_map/all_gather | solution.py:79
  197.6 2.4 convolution_convert_fusion.9
  200.1 7.1 all-gather
  207.2 11.8 %reduce-scatter.11.cloned.1.call-done = bf16[16,1536]{1,0:T(8,128)(2,1)} async-done(((bf16[64,1536]{1,0:T(8,128)(2,1)}), bf16[16,1536]{1,0:T(8,128)(2,1)}) %reduce-scatter.11.cloned.1.call-update) | async-done | bytes 49168 | tf_op jit(solution)/shard_map/while/body/eval_jaxpr/reduce_scatter | solution.py:146
  221.9 5.6 all_gather.40
  228.2 3.3 fusion.85
  231.5 4.0 fusion.8
  236.2 4.6 convolution_convert_fusion.7
  241.6 19.1 %reduce-scatter.15.cloned.1.call-done = bf16[16,1536]{1,0:T(8,128)(2,1)} async-done(((bf16[64,1536]{1,0:T(8,128)(2,1)}), bf16[16,1536]{1,0:T(8,128)(2,1)}) %reduce-scatter.15.cloned.1.call-update) | async-done | bytes 49168 | tf_op jit(solution)/shard_map/while/body/eval_jaxpr/reduce_scatter | solution.py:173
  263.2 5.6 all_gather.42
  269.4 2.5 convolution_convert_fusion.5
  272.6 22.0 %psum.7 = f32[]{:T(128)} all-reduce(f32[]{:T(128)S(6)} %add.196), channel_id=1, replica_groups=mesh['wide'=8,'narrow'=4] {'wide'}, use_global_device_ids=true, to_apply=%region_14.15 | all-reduce | flops 1 | bytes 8 | tf_op jit(solution)/shard_map/psum | solution.py:73
  295.4 4.2 multiply_reduce_fusion.4
  304.1 3.6 fusion.6
  313.9 2.9 convolution_convert_fusion.3
  316.8 10.9 %convolution_convert_fusion.4 = bf16[1536,768]{0,1:T(8,128)(2,1)} fusion(bf16[2112,1536]{1,0:T(8,128)(2,1)} %copy-done.6, bf16[2112,384]{0,1:T(8,128)(2,1)S(1)} %bitcast.160, bf16[2112,384]{0,1:T(8,128)(2,1)S(1)} %bitcast.155), kind=kOutput, calls=%fused_computation.19 | convolution fusion | flops 4990500864 | bytes 12091392 | tf_op jit(solution)/shard_map/while/body/eval_jaxpr/kd,ke->de/dot_general | solution.py:215
  327.7 6.9 copy.135
  335.3 3.5 fusion.7
  338.8 8.7 copy.126
  347.6 4.7 all-to-all-start
  352.3 4.7 convolution_convert_fusion.8
  357.3 31.9 %all-to-all-done = bf16[2048,2,384]{2,1,0:T(2,128)(2,1)} async-done(((bf16[2048,2,384]{2,1,0:T(2,128)(2,1)}), bf16[2048,2,384]{2,1,0:T(2,128)(2,1)}, u32[]{:S(2)}, u32[]{:S(2)}) %all-to-all-start) | async-done | bytes 3145760 | tf_op jit(solution)/shard_map/while/body/eval_jaxpr/all_to_all | solution.py:230
  393.5 10.0 %multiply_reduce_fusion = (f32[1536]{0:T(1024)}, f32[512]{0:T(512)S(1)}, f32[512]{0:T(512)S(1)}, f32[1536]{0:T(1024)}, f32[512,1536]{1,0:T(8,128)S(1)}) fusion(f32[512,1536]{1,0:T(8,128)S(1)} %get-tuple-element.150, f32[512]{0:T(512)S(1)} %add_rsqrt_fusion, f32[512]{0:T(512)S(1)} %broadcast_multiply_fusion.2, f32[1536]{0:T(1024)S(1)} %copy-done.33, ...), kind=kOutput, calls=%fused_computation.23 | convolution fusion | flops 4838912000 | bytes 18900992 | tf_op jit(solution)/shard_map/while/body/eval_jaxpr/rsc,dsc->rd/dot_general | solution.py:233
  405.6 3.6 convolution_bitcast_fusion.1
  409.3 3.5 convolution_convert_fusion.1
  413.9 3.9 convolution_convert_fusion
  421.3 3.6 all-to-all-start.1
  426.2 3.8 all-to-all-done.1
  431.6 31.3 %reduce-scatter.17.cloned.1.call-done = bf16[192,384]{1,0:T(8,128)(2,1)} async-done(((bf16[1536,384]{1,0:T(8,128)(2,1)}), bf16[192,384]{1,0:T(8,128)(2,1)}) %reduce-scatter.17.cloned.1.call-update) | async-done | bytes 147472 | tf_op jit(solution)/shard_map/reduce_scatter | solution.py:306
  464.6 109.4 %all-reduce.11.cloned.1.call-done = bf16[1536,2,384]{2,1,0:T(2,128)(2,1)} async-done(((bf16[1536,2,384]{2,1,0:T(2,128)(2,1)}), bf16[1536,2,384]{2,1,0:T(2,128)(2,1)}) %all-reduce.11.cloned.1.call-update) | async-done | bytes 2359312
  576.0 6.2 convolution_bitcast_fusion.2
  582.3 29.8 %all-gather.18.cloned.1.call-done = bf16[1536,1536]{1,0:T(8,128)(2,1)} async-done(((bf16[1536,384]{1,0:T(8,128)(2,1)}), bf16[1536,1536]{1,0:T(8,128)(2,1)}) %all-gather.18.cloned.1.call-update) | async-done | bytes 4718608 | tf_op jit(solution)/shard_map/all_gather | solution.py:82
  612.1 3.8 fusion.53
  616.0 40.1 %all-reduce.8 = (f32[1536]{0:T(1024)S(1)}, f32[1536]{0:T(1024)S(1)}, f32[1536]{0:T(1024)S(1)}, f32[1536]{0:T(1024)S(1)}, f32[1536]{0:T(1024)S(1)}, /*index=5*/f32[1536]{0:T(1024)S(1)}) all-reduce(f32[1536]{0:T(1024)S(1)} %copy-done.46, f32[1536]{0:T(1024)S(1)} %copy-done.47, ...), channel_id=7, replica_groups=mesh['wide'=8,'narrow'=4] {'wide','narrow'}, use_global_device_ids=true, to_apply=%region_23.24.clone | all-reduce | flops 9216 | bytes 73728
  661.2 74.4 %reduce-scatter.25.cloned.1.call-done = f32[48,8]{1,0:T(8,128)} async-done(((f32[1536,8]{1,0:T(8,128)}), f32[48,8]{1,0:T(8,128)}) %reduce-scatter.25.cloned.1.call-update) | async-done | bytes 1552
  737.0 96.9 %reduce-scatter.21.cloned.1.call-done = bf16[192,1536]{1,0:T(8,128)(2,1)} async-done(((bf16[1536,1536]{1,0:T(8,128)(2,1)}), bf16[192,1536]{1,0:T(8,128)(2,1)}) %reduce-scatter.21.cloned.1.call-update) | async-done | bytes 589840 | tf_op jit(solution)/shard_map/reduce_scatter | solution.py:300
  836.0 96.6 %reduce-scatter.23.cloned.1.call-done = bf16[1536,192]{0,1:T(8,128)(2,1)} async-done(((bf16[1536,1536]{0,1:T(8,128)(2,1)}), bf16[1536,192]{0,1:T(8,128)(2,1)}) %reduce-scatter.23.cloned.1.call-update) | async-done | bytes 589840 | tf_op jit(solution)/shard_map/reduce_scatter | solution.py:303
  (218 shorter events, 61.9 us)
Async XLA Ops:
  7.2 46.9 %all-gather.12.cloned.1.call-start = ((), (), s32[]{:S(2)}) async-start(), calls=%async_computation.12 | async-start | bytes 1327104 | tf_op jit(solution)/shard_map/all_gather | solution.py:77
  7.9 99.4 %all-gather.10.cloned.1.call-start = ((), (), s32[]{:S(2)}) async-start(), calls=%async_computation.11 | async-start | bytes 2654208 | tf_op jit(solution)/shard_map/all_gather | solution.py:78
  9.7 144.7 %all-gather.8.cloned.1.call-start = ((), (), s32[]{:S(2)}) async-start(), calls=%async_computation.10 | async-start | bytes 7864320 | tf_op jit(solution)/shard_map/while/body/eval_jaxpr/all_gather | solution.py:115
  12.5 10.4 %copy-start.45 = (s32[1,2048]{1,0:T(1,128)S(1)}, s32[1,2048]{1,0:T(1,128)}, u32[]{:S(2)}) copy-start(s32[1,2048]{1,0:T(1,128)} %param.20) | copy-start | bytes 24580
  14.2 183.4 %all-gather.14.cloned.1.call-start = ((), (), s32[]{:S(2)}) async-start(), calls=%async_computation.13 | async-start | bytes 1327104 | tf_op jit(solution)/shard_map/all_gather | solution.py:79
  14.8 204.2 %reduce-scatter.11.cloned.1.call-start = ((), (), s32[]{:S(2)}) async-start(), calls=%async_computation.14 | async-start | bytes 245760 | tf_op jit(solution)/shard_map/while/body/eval_jaxpr/reduce_scatter | solution.py:146
  15.0 7.9 copy-start.39
  15.2 7.6 copy-start.48
  23.5 149.4 %copy-start.54 = (pred[2112]{0:T(1024)(128)(4,1)}, pred[2112]{0:T(1024)(128)(4,1)S(1)}, u32[]{:S(2)}) copy-start(pred[2112]{0:T(1024)(128)(4,1)S(1)} %concatenate.18) | copy-start | bytes 6340
  55.8 117.2 %copy-start.27 = (bf16[64,4,96]{2,1,0:T(4,128)(2,1)}, bf16[64,4,96]{2,1,0:T(4,128)(2,1)S(1)}, u32[]{:S(2)}) copy-start(bf16[64,4,96]{2,1,0:T(4,128)(2,1)S(1)} %reshape.235) | copy-start | bytes 147460
  176.6 127.5 %copy-start.57 = (f32[4,64]{1,0:T(4,128)}, f32[4,64]{1,0:T(4,128)S(1)}, u32[]{:S(2)}) copy-start(f32[4,64]{1,0:T(4,128)S(1)} %get-tuple-element.151) | copy-start | bytes 3076
  176.6 44.4 %copy-start.28 = (f32[1536]{0:T(1024)S(1)}, f32[1536]{0:T(1024)}, u32[]{:S(2)}) copy-start(f32[1536]{0:T(1024)} %param.26) | copy-start | bytes 18436
  176.6 44.4 %copy-start.44 = (f32[1536]{0:T(1024)S(1)}, f32[1536]{0:T(1024)}, u32[]{:S(2)}) copy-start(f32[1536]{0:T(1024)} %param.27) | copy-start | bytes 18436
  181.3 50.1 %copy-start.18 = (f32[64,384]{1,0:T(8,128)}, f32[64,384]{1,0:T(8,128)S(1)}, u32[]{:S(2)}) copy-start(f32[64,384]{1,0:T(8,128)S(1)} %reshape.237) | copy-start | bytes 294916
  200.1 60.6 %reduce-scatter.15.cloned.1.call-start = ((), (), s32[]{:S(2)}) async-start(), calls=%async_computation.16 | async-start | bytes 245760 | tf_op jit(solution)/shard_map/while/body/eval_jaxpr/reduce_scatter | solution.py:173
  219.0 12.5 %copy-start.22 = (bf16[1,64,1536]{2,1,0:T(8,128)(2,1)S(1)}, bf16[1,64,1536]{2,1,0:T(8,128)(2,1)}, u32[]{:S(2)}) copy-start(bf16[1,64,1536]{2,1,0:T(8,128)(2,1)} %all-gather) | copy-start | bytes 589828
  220.0 42.3 %copy-start.36 = (f32[16]{0:T(128)}, f32[16]{0:T(128)S(1)}, u32[]{:S(2)}) copy-start(f32[16]{0:T(128)S(1)} %broadcast_multiply_fusion.7) | copy-start | bytes 196
  221.0 41.2 %copy-start.41 = (f32[16]{0:T(128)}, f32[16]{0:T(128)S(1)}, u32[]{:S(2)}) copy-start(f32[16]{0:T(128)S(1)} %add_rsqrt_fusion.1) | copy-start | bytes 196
  236.2 24.5 %copy-start.17 = (bf16[16,1536]{1,0:T(8,128)(2,1)S(1)}, bf16[16,1536]{1,0:T(8,128)(2,1)}, u32[]{:S(2)}) copy-start(bf16[16,1536]{1,0:T(8,128)(2,1)} %reduce-scatter.11.cloned.1.call-done) | copy-start | bytes 147460
  236.2 26.1 %copy-start.25 = (bf16[1,16,1536]{2,1,0:T(8,128)(2,1)S(1)}, bf16[1,16,1536]{2,1,0:T(8,128)(2,1)}, u32[]{:S(2)}) copy-start(bf16[1,16,1536]{2,1,0:T(8,128)(2,1)} %param.33) | copy-start | bytes 147460
  240.8 54.6 %copy-start.55 = (pred[2112]{0:T(1024)(128)(4,1)S(1)}, pred[2112]{0:T(1024)(128)(4,1)}, u32[]{:S(2)}) copy-start(pred[2112]{0:T(1024)(128)(4,1)} %copy-done.54) | copy-start | bytes 6340
  240.8 152.7 %all-gather.16.cloned.1.call-start = ((), (), s32[]{:S(2)}) async-start(), calls=%async_computation.17 | async-start | bytes 11796480 | tf_op jit(solution)/shard_map/all_gather | solution.py:83
  241.5 188.5 %reduce-scatter.19.cloned.1.call-start = ((), (), s32[]{:S(2)}) async-start(), calls=%async_computation.20 | async-start | bytes 1327104 | tf_op jit(solution)/shard_map/reduce_scatter | solution.py:315
  262.2 37.3 %copy-start.50 = (f32[16]{0:T(128)}, f32[16]{0:T(128)S(1)}, u32[]{:S(2)}) copy-start(f32[16]{0:T(128)S(1)} %get-tuple-element.159) | copy-start | bytes 196
  262.2 37.3 %copy-start.52 = (f32[16]{0:T(128)}, f32[16]{0:T(128)S(1)}, u32[]{:S(2)}) copy-start(f32[16]{0:T(128)S(1)} %get-tuple-element.160) | copy-start | bytes 196
  271.9 191.0 %reduce-scatter.17.cloned.1.call-start = ((), (), s32[]{:S(2)}) async-start(), calls=%async_computation.19 | async-start | bytes 1327104 | tf_op jit(solution)/shard_map/reduce_scatter | solution.py:306
  311.9 262.1 %all-reduce.11.cloned.1.call-start = ((), (), s32[]{:S(2)}) async-start(), calls=%async_computation.24 | async-start | bytes 4718592
  316.8 11.0 %copy-start.4 = (bf16[4,96,2112]{2,1,0:T(8,128)(2,1)}, bf16[4,96,2112]{2,1,0:T(8,128)(2,1)S(1)}, u32[]{:S(2)}) copy-start(bf16[4,96,2112]{2,1,0:T(8,128)(2,1)S(1)} %convolution_convert_fusion.3) | copy-start | bytes 4866052
  334.6 277.5 %all-gather.18.cloned.1.call-start = ((), (), s32[]{:S(2)}) async-start(), calls=%async_computation.18 | async-start | bytes 5898240 | tf_op jit(solution)/shard_map/all_gather | solution.py:82
  347.6 41.7 %all-to-all-start = ((bf16[2048,2,384]{2,1,0:T(2,128)(2,1)}), bf16[2048,2,384]{2,1,0:T(2,128)(2,1)}, u32[]{:S(2)}, u32[]{:S(2)}) async-start(bf16[2048,2,384]{2,1,0:T(2,128)(2,1)} %copy.126), calls=%async_computation.3 | async-start | bytes 6291456 | tf_op jit(solution)/shard_map/while/body/eval_jaxpr/all_to_all | solution.py:230
  352.3 307.3 %reduce-scatter.13.cloned.1.call-start = ((), (), s32[]{:S(2)}) async-start(), calls=%async_computation.15 | async-start | bytes 245760 | tf_op jit(solution)/shard_map/while/body/eval_jaxpr/reduce_scatter | solution.py:158
  357.0 378.5 %reduce-scatter.25.cloned.1.call-start = ((), (), s32[]{:S(2)}) async-start(), calls=%async_computation.23 | async-start | bytes 811008
  409.3 424.6 %reduce-scatter.21.cloned.1.call-start = ((), (), s32[]{:S(2)}) async-start(), calls=%async_computation.21 | async-start | bytes 5308416 | tf_op jit(solution)/shard_map/reduce_scatter | solution.py:300
  412.9 519.8 %reduce-scatter.23.cloned.1.call-start = ((), (), s32[]{:S(2)}) async-start(), calls=%async_computation.22 | async-start | bytes 5308416 | tf_op jit(solution)/shard_map/reduce_scatter | solution.py:303
  417.8 7.1 copy-start.56
  421.3 8.6 all-to-all-start.1
  576.0 36.2 %copy-start.40 = (f32[16]{0:T(128)S(1)}, f32[16]{0:T(128)}, u32[]{:S(2)}) copy-start(f32[16]{0:T(128)} %copy-done.39) | copy-start | bytes 196
  576.0 36.2 %copy-start.49 = (f32[16]{0:T(128)S(1)}, f32[16]{0:T(128)}, u32[]{:S(2)}) copy-start(f32[16]{0:T(128)} %copy-done.48) | copy-start | bytes 196
  582.2 33.7 %copy-start.31 = (f32[1536]{0:T(1024)S(1)}, f32[1536]{0:T(1024)}, u32[]{:S(2)}) copy-start(f32[1536]{0:T(1024)} %get-tuple-element.98) | copy-start | bytes 18436
  582.2 33.8 %copy-start.46 = (f32[1536]{0:T(1024)S(1)}, f32[1536]{0:T(1024)}, u32[]{:S(2)}) copy-start(f32[1536]{0:T(1024)} %get-tuple-element.87) | copy-start | bytes 18436
  582.2 33.8 %copy-start.47 = (f32[1536]{0:T(1024)S(1)}, f32[1536]{0:T(1024)}, u32[]{:S(2)}) copy-start(f32[1536]{0:T(1024)} %get-tuple-element.90) | copy-start | bytes 18436
  582.2 77.3 %copy-start.24 = (bf16[16,1536]{1,0:T(8,128)(2,1)S(1)}, bf16[16,1536]{1,0:T(8,128)(2,1)}, u32[]{:S(2)}) copy-start(bf16[16,1536]{1,0:T(8,128)(2,1)} %reduce-scatter.15.cloned.1.call-done) | copy-start | bytes 147460
  582.2 77.3 %copy-start.26 = (bf16[1,16,1536]{2,1,0:T(8,128)(2,1)S(1)}, bf16[1,16,1536]{2,1,0:T(8,128)(2,1)}, u32[]{:S(2)}) copy-start(bf16[1,16,1536]{2,1,0:T(8,128)(2,1)} %param.33) | copy-start | bytes 147460
  582.3 77.3 %copy-start.37 = (f32[16]{0:T(128)S(1)}, f32[16]{0:T(128)}, u32[]{:S(2)}) copy-start(f32[16]{0:T(128)} %copy-done.36) | copy-start | bytes 196
  582.3 77.3 %copy-start.42 = (f32[16]{0:T(128)S(1)}, f32[16]{0:T(128)}, u32[]{:S(2)}) copy-start(f32[16]{0:T(128)} %copy-done.41) | copy-start | bytes 196
  582.3 77.3 %copy-start.51 = (f32[16]{0:T(128)S(1)}, f32[16]{0:T(128)}, u32[]{:S(2)}) copy-start(f32[16]{0:T(128)} %copy-done.50) | copy-start | bytes 196
  582.3 77.3 %copy-start.53 = (f32[16]{0:T(128)S(1)}, f32[16]{0:T(128)}, u32[]{:S(2)}) copy-start(f32[16]{0:T(128)} %copy-done.52) | copy-start | bytes 196
  612.1 322.7 %copy-start.1 = (bf16[8,1536]{1,0:T(8,128)(2,1)S(1)}, bf16[8,1536]{1,0:T(8,128)(2,1)}, u32[]{:S(2)}) copy-start(bf16[8,1536]{1,0:T(8,128)(2,1)} %param.21) | copy-start | bytes 73732
  (28 other events, 75.4 us)
Sparse Core Ops, SparseCore 0:
  10.2 43.8 all-gather.11
  56.8 50.4 all-gather.9
  109.5 44.8 all-gather.7
  156.5 41.1 all-gather.13
  200.5 18.4 reduce-scatter.10
  240.9 19.7 reduce-scatter.14
  262.3 64.0 all-gather.15
  330.4 64.8 reduce-scatter.18
  399.2 63.7 reduce-scatter.16
  466.4 107.5 all-reduce.10
  575.6 36.5 all-gather.17
  614.4 19.8 reduce-scatter.12
  639.4 96.1 reduce-scatter.24
  739.1 94.7 reduce-scatter.20
  837.3 95.2 reduce-scatter.22
where the time goes:
time: 944 us; the launch traced here: 941 us
  waiting for transfers between devices  649 us (69%)
  matrix products  95.8 us (10%)
  blocking collectives  87.2 us (9%)
  local copies, waits for them, and re-layouts  54.7 us (6%)
  other arithmetic  28.2 us (3%)
  between operations  17.4 us (2%)
    unnamed x17, waiting for transfers between devices  187 us
    reduce_scatter x1, waiting for transfers between devices, body(): lax.psum_scatter(up_acc.astype(jnp.bfloat16), 'wide', scatter_dimension=0...  96.9 us
    reduce_scatter x1, waiting for transfers between devices, body(): lax.psum_scatter(down_acc.astype(jnp.bfloat16), 'wide', scatter_dimension...  96.6 us
    all_gather x1, waiting for transfers between devices, body(): lax.all_gather(keyval_weight, 'wide', axis=0, tiled=True)  51.6 us
    all_gather x1, waiting for transfers between devices, item_step(): lax.all_gather(media_nf.astype(jnp.bfloat16), 'narrow', axis=0, tiled=True)  42.8 us
    unnamed x1, blocking collectives  40.1 us
    all_to_all x1, waiting for transfers between devices, item_step(): lax.all_to_all(media_pairs, 'narrow', split_axis=0, concat_axis=2, tiled=...  31.9 us
    reduce_scatter x1, waiting for transfers between devices, body(): lax.psum_scatter(query_acc.astype(jnp.bfloat16), 'wide', scatter_dimensio...  31.3 us
  transfers between devices with their start and end apart: 17, of which 14 were waited for; matrix products, arithmetic and copies ran while one was open for 16% of the time, Pallas kernels for 0%

commit v1 on v0

--- a/solution.py
+++ b/solution.py
@@ -11,6 +11,16 @@
 EPS = 1e-05
 ENT_COEF = 4.0
 HIGH = lax.Precision.HIGHEST
+
+
+def mix_pages_up(local_values, array_axis):
+    local_values = jnp.moveaxis(local_values, 0, array_axis)
+    state_now = local_values.shape
+    return local_values.reshape(
+        *state_now[:array_axis],
+        state_now[array_axis] * state_now[array_axis + 1],
+        *state_now[array_axis + 2 :]
+    )
 
 
 def norm_forward(values, norm_gain, norm_bias):
@@ -73,8 +83,36 @@
     total_count = lax.psum(local_count, "wide")
     all_items = item_count * lax.axis_size("wide")
     ent_weight = ENT_COEF * float(all_items * media_total) / total_count
+
+    def floor_guide(inner_x, which_axis, dim_no):
+        n_lanes = lax.axis_size(which_axis)
+        nodes = []
+        dev = 0
+        while dev < n_lanes:
+            nodes.append((dev, (dev + 1) % n_lanes))
+            dev += 1
+        made = []
+        for b, num in nodes:
+            made.append((num, b))
+        long_array, big = ([], [])
+        nth = 0
+        while nth < n_lanes - 1:
+            if nth % 2 == 0:
+                long_array.append(
+                    lax.ppermute(long_array[-1] if long_array else inner_x, which_axis, perm=nodes)
+                )
+            else:
+                val = lax.ppermute(big[-1] if big else inner_x, which_axis, perm=made)
+                big.append(val)
+            nth += 1
+        s_next = jnp.stack([*long_array[::-1], inner_x, *big], 0)
+        m_next = lax.axis_index(which_axis)
+        z_new = m_next - len(long_array)
+        s_next = s_next[(jnp.arange(n_lanes) - z_new) % n_lanes]
+        return mix_pages_up(s_next, dim_no)
+
     query_own, keyval_own, output_own = (
-        lax.all_gather(query_weight, "wide", axis=0, tiled=True),
+        floor_guide(query_weight, "wide", 0),
         lax.all_gather(keyval_weight, "wide", axis=0, tiled=True),
         lax.all_gather(output_weight, "wide", axis=1, tiled=True),
     )

time: 944 us -> 911 us (0.965)
  waiting for transfers between devices: 649 us -> 586 us
  starting transfers between devices: 9.14 us -> 27.4 us
  local copies, waits for them, and re-layouts: 54.7 us -> 70.3 us
    all_gather x1, waiting for transfers between devices: 51.6 us -> 0.02 us  [body(): lax.all_gather(keyval_weight, 'wide', axis=0, tiled=True)]
    all_gather x1 -> x0, waiting for transfers between devices: 30.5 us -> none  [body(): lax.all_gather(query_weight, 'wide', axis=0, tiled=True)]
    ppermute x0 -> x7, starting transfers between devices: none -> 18.3 us  [the longest x3 12.6 us: floor_guide(): val = lax.ppermute(big[-1] if big else inner_x, which_axis, perm=made)]
    ppermute x0 -> x7, waiting for transfers between devices: none -> 16.9 us  [the longest x4 16.9 us: floor_guide(): lax.ppermute(long_array[-1] if long_array else inner_x, which_axis, perm=...]
    unnamed x128 -> x137, local copies, waits for them, and re-layouts: 15.5 us -> 27.4 us
    unnamed x17 -> x16, waiting for transfers between devices: 187 us -> 185 us
  transfers between devices with their start and end apart: 17 -> 23, of which waited for: 14 -> 16; matrix products, arithmetic and copies ran while one was open for 16% -> 18% of each run, Pallas kernels for 0% -> 0%
where the time goes in v1:
time: 911 us; the launch traced here: 908 us
  waiting for transfers between devices  586 us (64%)
  matrix products  93.2 us (10%)
  blocking collectives  86.1 us (9%)
  local copies, waits for them, and re-layouts  70.3 us (8%)
  other arithmetic  28.3 us (3%)
  starting transfers between devices  27.4 us (3%)
  between operations  17.4 us (2%)
    unnamed x16, waiting for transfers between devices  185 us
    reduce_scatter x1, waiting for transfers between devices, body(): lax.psum_scatter(up_acc.astype(jnp.bfloat16), 'wide', scatter_dimension=0...  97 us
    reduce_scatter x1, waiting for transfers between devices, body(): lax.psum_scatter(down_acc.astype(jnp.bfloat16), 'wide', scatter_dimension...  96.6 us
    all_gather x1, waiting for transfers between devices, item_step(): lax.all_gather(media_nf.astype(jnp.bfloat16), 'narrow', axis=0, tiled=True)  43.9 us
    unnamed x1, blocking collectives  40.1 us
    reduce_scatter x1, waiting for transfers between devices, body(): lax.psum_scatter(query_acc.astype(jnp.bfloat16), 'wide', scatter_dimensio...  32.6 us
    all_to_all x1, waiting for transfers between devices, item_step(): lax.all_to_all(media_pairs, 'narrow', split_axis=0, concat_axis=2, tiled=...  31.9 us
    all_gather x1, waiting for transfers between devices, body(): lax.all_gather(query_own, 'narrow', axis=1, tiled=True)  30.3 us
  transfers between devices with their start and end apart: 23, of which 16 were waited for; matrix products, arithmetic and copies ran while one was open for 18% of the time, Pallas kernels for 0%

profile of v1, /device:TPU:0, one launch (start us, length us, event | category | flops | bytes accessed | tf_op | source)
XLA Modules:
  0.0 908.3 jit_solution(5497624061497213550)
XLA Ops:
  13.7 3.0 collective-permute-start
  16.8 3.1 collective-permute-start.4
  20.3 5.0 collective-permute-done
  28.6 8.2 collective-permute-done.1
  37.5 4.8 collective-permute-start.5
  45.0 5.6 all_gather.33
  50.7 4.8 collective-permute-start.6
  73.0 4.3 copy.117
  77.2 43.9 %all-gather.7.cloned.1.call-done = bf16[2048,1536]{1,0:T(8,128)(2,1)} async-done(((bf16[512,1536]{1,0:T(8,128)(2,1)}), bf16[2048,1536]{1,0:T(8,128)(2,1)}) %all-gather.7.cloned.1.call-update) | async-done | bytes 6291472 | tf_op jit(solution)/shard_map/while/body/eval_jaxpr/all_gather | solution.py:153
  121.1 3.3 constant_dynamic-update-slice_fusion.1
  124.6 5.5 convolution_convert_fusion.2
  132.1 3.8 copy.119
  135.9 3.8 copy.118
  139.7 3.6 fusion.84
  148.0 16.5 %all-gather.11.cloned.1.call-done = bf16[384,1536]{0,1:T(8,128)(2,1)} async-done(((bf16[384,192]{0,1:T(8,128)(2,1)}), bf16[384,1536]{0,1:T(8,128)(2,1)}) %all-gather.11.cloned.1.call-update) | async-done | bytes 1179664 | tf_op jit(solution)/shard_map/all_gather | solution.py:117
  167.0 7.1 all-gather
  174.1 11.8 %reduce-scatter.11.cloned.1.call-done = bf16[16,1536]{1,0:T(8,128)(2,1)} async-done(((bf16[64,1536]{1,0:T(8,128)(2,1)}), bf16[16,1536]{1,0:T(8,128)(2,1)}) %reduce-scatter.11.cloned.1.call-update) | async-done | bytes 49168 | tf_op jit(solution)/shard_map/while/body/eval_jaxpr/reduce_scatter | solution.py:184
  188.7 5.6 all_gather.36
  195.0 3.3 fusion.87
  198.3 4.0 fusion.8
  203.1 4.6 convolution_convert_fusion.7
  208.3 19.3 %reduce-scatter.15.cloned.1.call-done = bf16[16,1536]{1,0:T(8,128)(2,1)} async-done(((bf16[64,1536]{1,0:T(8,128)(2,1)}), bf16[16,1536]{1,0:T(8,128)(2,1)}) %reduce-scatter.15.cloned.1.call-update) | async-done | bytes 49168 | tf_op jit(solution)/shard_map/while/body/eval_jaxpr/reduce_scatter | solution.py:211
  230.0 5.8 all_gather.38
  239.7 21.9 %psum.7 = f32[]{:T(128)} all-reduce(f32[]{:T(128)S(6)} %add.222), channel_id=1, replica_groups=mesh['wide'=8,'narrow'=4] {'wide'}, use_global_device_ids=true, to_apply=%region_14.15 | all-reduce | flops 1 | bytes 8 | tf_op jit(solution)/shard_map/psum | solution.py:83
  262.3 4.2 multiply_reduce_fusion.4
  271.0 3.6 fusion.6
  282.2 10.4 %convolution_convert_fusion.4 = bf16[1536,768]{0,1:T(8,128)(2,1)} fusion(bf16[2112,1536]{1,0:T(8,128)(2,1)} %copy-done.6, bf16[2112,384]{0,1:T(8,128)(2,1)S(1)} %bitcast.181, bf16[2112,384]{0,1:T(8,128)(2,1)S(1)} %bitcast.174), kind=kOutput, calls=%fused_computation.20 | convolution fusion | flops 4990500864 | bytes 12091392 | tf_op jit(solution)/shard_map/while/body/eval_jaxpr/kd,ke->de/dot_general | solution.py:253
  292.6 6.9 copy.135
  300.1 3.5 fusion.7
  303.6 8.8 copy.126
  312.4 4.7 all-to-all-start
  317.1 4.7 convolution_convert_fusion.8
  322.1 31.9 %all-to-all-done = bf16[2048,2,384]{2,1,0:T(2,128)(2,1)} async-done(((bf16[2048,2,384]{2,1,0:T(2,128)(2,1)}), bf16[2048,2,384]{2,1,0:T(2,128)(2,1)}, u32[]{:S(2)}, u32[]{:S(2)}) %all-to-all-start) | async-done | bytes 3145760 | tf_op jit(solution)/shard_map/while/body/eval_jaxpr/all_to_all | solution.py:268
  358.3 10.0 %multiply_reduce_fusion = (f32[1536]{0:T(1024)}, f32[512]{0:T(512)S(1)}, f32[512]{0:T(512)S(1)}, f32[1536]{0:T(1024)}, f32[512,1536]{1,0:T(8,128)S(1)}) fusion(f32[512,1536]{1,0:T(8,128)S(1)} %get-tuple-element.150, f32[512]{0:T(512)S(1)} %add_rsqrt_fusion, f32[512]{0:T(512)S(1)} %broadcast_multiply_fusion.2, f32[1536]{0:T(1024)S(1)} %copy-done.33, ...), kind=kOutput, calls=%fused_computation.24 | convolution fusion | flops 4838912000 | bytes 18900992 | tf_op jit(solution)/shard_map/while/body/eval_jaxpr/rsc,dsc->rd/dot_general | solution.py:271
  370.3 3.6 convolution_bitcast_fusion.1
  374.1 3.5 convolution_convert_fusion.1
  378.7 3.9 convolution_convert_fusion
  386.1 3.6 all-to-all-start.1
  391.0 3.8 all-to-all-done.1
  396.4 32.6 %reduce-scatter.17.cloned.1.call-done = bf16[192,384]{1,0:T(8,128)(2,1)} async-done(((bf16[1536,384]{1,0:T(8,128)(2,1)}), bf16[192,384]{1,0:T(8,128)(2,1)}) %reduce-scatter.17.cloned.1.call-update) | async-done | bytes 147472 | tf_op jit(solution)/shard_map/reduce_scatter | solution.py:344
  430.7 109.6 %all-reduce.11.cloned.1.call-done = bf16[1536,2,384]{2,1,0:T(2,128)(2,1)} async-done(((bf16[1536,2,384]{2,1,0:T(2,128)(2,1)}), bf16[1536,2,384]{2,1,0:T(2,128)(2,1)}) %all-reduce.11.cloned.1.call-update) | async-done | bytes 2359312
  542.2 6.2 convolution_bitcast_fusion.2
  548.6 30.3 %all-gather.15.cloned.1.call-done = bf16[1536,1536]{1,0:T(8,128)(2,1)} async-done(((bf16[1536,384]{1,0:T(8,128)(2,1)}), bf16[1536,1536]{1,0:T(8,128)(2,1)}) %all-gather.15.cloned.1.call-update) | async-done | bytes 4718608 | tf_op jit(solution)/shard_map/all_gather | solution.py:120
  578.8 3.8 fusion.53
  582.7 40.1 %all-reduce.8 = (f32[1536]{0:T(1024)S(1)}, f32[1536]{0:T(1024)S(1)}, f32[1536]{0:T(1024)S(1)}, f32[1536]{0:T(1024)S(1)}, f32[1536]{0:T(1024)S(1)}, /*index=5*/f32[1536]{0:T(1024)S(1)}) all-reduce(f32[1536]{0:T(1024)S(1)} %copy-done.46, f32[1536]{0:T(1024)S(1)} %copy-done.47, ...), channel_id=7, replica_groups=mesh['wide'=8,'narrow'=4] {'wide','narrow'}, use_global_device_ids=true, to_apply=%region_23.24.clone | all-reduce | flops 9216 | bytes 73728
  627.9 74.4 %reduce-scatter.25.cloned.1.call-done = f32[48,8]{1,0:T(8,128)} async-done(((f32[1536,8]{1,0:T(8,128)}), f32[48,8]{1,0:T(8,128)}) %reduce-scatter.25.cloned.1.call-update) | async-done | bytes 1552
  703.8 97.0 %reduce-scatter.21.cloned.1.call-done = bf16[192,1536]{1,0:T(8,128)(2,1)} async-done(((bf16[1536,1536]{1,0:T(8,128)(2,1)}), bf16[192,1536]{1,0:T(8,128)(2,1)}) %reduce-scatter.21.cloned.1.call-update) | async-done | bytes 589840 | tf_op jit(solution)/shard_map/reduce_scatter | solution.py:338
  803.0 96.6 %reduce-scatter.23.cloned.1.call-done = bf16[1536,192]{0,1:T(8,128)(2,1)} async-done(((bf16[1536,1536]{0,1:T(8,128)(2,1)}), bf16[1536,192]{0,1:T(8,128)(2,1)}) %reduce-scatter.23.cloned.1.call-update) | async-done | bytes 589840 | tf_op jit(solution)/shard_map/reduce_scatter | solution.py:341
  (242 shorter events, 90.8 us)
Async XLA Ops:
  7.2 65.8 %all-gather.9.cloned.1.call-start = ((), (), s32[]{:S(2)}) async-start(), calls=%async_computation.11 | async-start | bytes 2654208 | tf_op jit(solution)/shard_map/all_gather | solution.py:116
  9.0 112.2 %all-gather.7.cloned.1.call-start = ((), (), s32[]{:S(2)}) async-start(), calls=%async_computation.10 | async-start | bytes 7864320 | tf_op jit(solution)/shard_map/while/body/eval_jaxpr/all_gather | solution.py:153
  11.9 24.9 %copy-start.45 = (s32[1,2048]{1,0:T(1,128)S(1)}, s32[1,2048]{1,0:T(1,128)}, u32[]{:S(2)}) copy-start(s32[1,2048]{1,0:T(1,128)} %param.20) | copy-start | bytes 24580
  13.7 150.8 %all-gather.11.cloned.1.call-start = ((), (), s32[]{:S(2)}) async-start(), calls=%async_computation.12 | async-start | bytes 1327104 | tf_op jit(solution)/shard_map/all_gather | solution.py:117
  13.7 11.6 %collective-permute-start = (bf16[192,384]{1,0:T(8,128)(2,1)S(1)}, bf16[192,384]{1,0:T(8,128)(2,1)}, u32[]{:S(2)}, u32[]{:S(2)}) collective-permute-start(bf16[192,384]{1,0:T(8,128)(2,1)S(1)} %copy-done.28), channel_id=1, source_target_pairs={{0,4},{4,8},{8,12},{12,16},{16,20},{20,24},{24,28},{28,0},{1,5},{5... | collective-permute-start | bytes 442376 | tf_op jit(solution)/shard_map/ppermute | solution.py:102
  16.8 20.7 %collective-permute-start.4 = (bf16[192,384]{1,0:T(8,128)(2,1)S(1)}, bf16[192,384]{1,0:T(8,128)(2,1)}, u32[]{:S(2)}, u32[]{:S(2)}) collective-permute-start(bf16[192,384]{1,0:T(8,128)(2,1)S(1)} %copy-done.28), channel_id=1, source_target_pairs={{4,0},{8,4},{12,8},{16,12},{20,16},{24,20},{28,24},{0,28},{5,1},{9... | collective-permute-start | bytes 442376 | tf_op jit(solution)/shard_map/ppermute | solution.py:105
  19.9 166.0 %reduce-scatter.11.cloned.1.call-start = ((), (), s32[]{:S(2)}) async-start(), calls=%async_computation.13 | async-start | bytes 245760 | tf_op jit(solution)/shard_map/while/body/eval_jaxpr/reduce_scatter | solution.py:184
  25.3 11.5 %collective-permute-start.1 = (bf16[192,384]{1,0:T(8,128)(2,1)}, bf16[192,384]{1,0:T(8,128)(2,1)}, u32[]{:S(2)}, u32[]{:S(2)}) collective-permute-start(bf16[192,384]{1,0:T(8,128)(2,1)} %collective-permute-done), channel_id=1, source_target_pairs={{0,4},{4,8},{8,12},{12,16},{16,20},{20,24},{24,28},{28,0},{1,5},{5... | collective-permute-start | bytes 442376 | tf_op jit(solution)/shard_map/ppermute | solution.py:102
  36.8 8.2 collective-permute-start.2
  37.5 13.1 %collective-permute-start.5 = (bf16[192,384]{1,0:T(8,128)(2,1)}, bf16[192,384]{1,0:T(8,128)(2,1)}, u32[]{:S(2)}, u32[]{:S(2)}) collective-permute-start(bf16[192,384]{1,0:T(8,128)(2,1)} %collective-permute-done.4), channel_id=1, source_target_pairs={{4,0},{8,4},{12,8},{16,12},{20,16},{24,20},{28,24},{0,28},{5,1},{9... | collective-permute-start | bytes 442376 | tf_op jit(solution)/shard_map/ppermute | solution.py:105
  45.0 11.4 %collective-permute-start.3 = (bf16[192,384]{1,0:T(8,128)(2,1)}, bf16[192,384]{1,0:T(8,128)(2,1)}, u32[]{:S(2)}, u32[]{:S(2)}) collective-permute-start(bf16[192,384]{1,0:T(8,128)(2,1)} %collective-permute-done.2), channel_id=1, source_target_pairs={{0,4},{4,8},{8,12},{12,16},{16,20},{20,24},{24,28},{28,0},{1,5},{5... | collective-permute-start | bytes 442376 | tf_op jit(solution)/shard_map/ppermute | solution.py:102
  50.6 89.0 %copy-start.54 = (pred[2112]{0:T(1024)(128)(4,1)}, pred[2112]{0:T(1024)(128)(4,1)S(1)}, u32[]{:S(2)}) copy-start(pred[2112]{0:T(1024)(128)(4,1)S(1)} %concatenate.18) | copy-start | bytes 6340
  50.7 16.9 %collective-permute-start.6 = (bf16[192,384]{1,0:T(8,128)(2,1)}, bf16[192,384]{1,0:T(8,128)(2,1)S(1)}, u32[]{:S(2)}, u32[]{:S(2)}) collective-permute-start(bf16[192,384]{1,0:T(8,128)(2,1)} %collective-permute-done.5), channel_id=1, source_target_pairs={{4,0},{8,4},{12,8},{16,12},{20,16},{24,20},{28,24},{0,28},{5,1},{9... | collective-permute-start | bytes 442376 | tf_op jit(solution)/shard_map/ppermute | solution.py:105
  72.9 66.7 %copy-start.27 = (bf16[64,4,96]{2,1,0:T(4,128)(2,1)}, bf16[64,4,96]{2,1,0:T(4,128)(2,1)S(1)}, u32[]{:S(2)}) copy-start(bf16[64,4,96]{2,1,0:T(4,128)(2,1)S(1)} %reshape.288) | copy-start | bytes 147460
  146.2 41.6 %copy-start.29 = (f32[1536]{0:T(1024)S(1)}, f32[1536]{0:T(1024)}, u32[]{:S(2)}) copy-start(f32[1536]{0:T(1024)} %param.26) | copy-start | bytes 18436
  146.2 41.6 %copy-start.44 = (f32[1536]{0:T(1024)S(1)}, f32[1536]{0:T(1024)}, u32[]{:S(2)}) copy-start(f32[1536]{0:T(1024)} %param.27) | copy-start | bytes 18436
  148.0 50.3 %copy-start.18 = (f32[64,384]{1,0:T(8,128)}, f32[64,384]{1,0:T(8,128)S(1)}, u32[]{:S(2)}) copy-start(f32[64,384]{1,0:T(8,128)S(1)} %reshape.290) | copy-start | bytes 294916
  167.0 60.6 %reduce-scatter.15.cloned.1.call-start = ((), (), s32[]{:S(2)}) async-start(), calls=%async_computation.15 | async-start | bytes 245760 | tf_op jit(solution)/shard_map/while/body/eval_jaxpr/reduce_scatter | solution.py:211
  186.8 42.3 %copy-start.36 = (f32[16]{0:T(128)}, f32[16]{0:T(128)S(1)}, u32[]{:S(2)}) copy-start(f32[16]{0:T(128)S(1)} %broadcast_multiply_fusion.7) | copy-start | bytes 196
  187.8 41.3 %copy-start.41 = (f32[16]{0:T(128)}, f32[16]{0:T(128)S(1)}, u32[]{:S(2)}) copy-start(f32[16]{0:T(128)S(1)} %add_rsqrt_fusion.1) | copy-start | bytes 196
  207.6 20.0 %copy-start.17 = (bf16[16,1536]{1,0:T(8,128)(2,1)S(1)}, bf16[16,1536]{1,0:T(8,128)(2,1)}, u32[]{:S(2)}) copy-start(bf16[16,1536]{1,0:T(8,128)(2,1)} %reduce-scatter.11.cloned.1.call-done) | copy-start | bytes 147460
  207.6 21.5 %copy-start.25 = (bf16[1,16,1536]{2,1,0:T(8,128)(2,1)S(1)}, bf16[1,16,1536]{2,1,0:T(8,128)(2,1)}, u32[]{:S(2)}) copy-start(bf16[1,16,1536]{2,1,0:T(8,128)(2,1)} %param.33) | copy-start | bytes 147460
  207.6 150.6 %all-gather.13.cloned.1.call-start = ((), (), s32[]{:S(2)}) async-start(), calls=%async_computation.16 | async-start | bytes 11796480 | tf_op jit(solution)/shard_map/all_gather | solution.py:121
  208.2 54.0 %copy-start.55 = (pred[2112]{0:T(1024)(128)(4,1)S(1)}, pred[2112]{0:T(1024)(128)(4,1)}, u32[]{:S(2)}) copy-start(pred[2112]{0:T(1024)(128)(4,1)} %copy-done.54) | copy-start | bytes 6340
  208.2 186.5 %reduce-scatter.19.cloned.1.call-start = ((), (), s32[]{:S(2)}) async-start(), calls=%async_computation.19 | async-start | bytes 1327104 | tf_op jit(solution)/shard_map/reduce_scatter | solution.py:353
  229.1 37.4 %copy-start.50 = (f32[16]{0:T(128)}, f32[16]{0:T(128)S(1)}, u32[]{:S(2)}) copy-start(f32[16]{0:T(128)S(1)} %get-tuple-element.159) | copy-start | bytes 196
  229.1 37.4 %copy-start.52 = (f32[16]{0:T(128)}, f32[16]{0:T(128)S(1)}, u32[]{:S(2)}) copy-start(f32[16]{0:T(128)S(1)} %get-tuple-element.160) | copy-start | bytes 196
  239.0 190.1 %reduce-scatter.17.cloned.1.call-start = ((), (), s32[]{:S(2)}) async-start(), calls=%async_computation.18 | async-start | bytes 1327104 | tf_op jit(solution)/shard_map/reduce_scatter | solution.py:344
  278.7 261.5 %all-reduce.11.cloned.1.call-start = ((), (), s32[]{:S(2)}) async-start(), calls=%async_computation.23 | async-start | bytes 4718592
  299.5 279.3 %all-gather.15.cloned.1.call-start = ((), (), s32[]{:S(2)}) async-start(), calls=%async_computation.17 | async-start | bytes 5898240 | tf_op jit(solution)/shard_map/all_gather | solution.py:120
  312.4 41.6 %all-to-all-start = ((bf16[2048,2,384]{2,1,0:T(2,128)(2,1)}), bf16[2048,2,384]{2,1,0:T(2,128)(2,1)}, u32[]{:S(2)}, u32[]{:S(2)}) async-start(bf16[2048,2,384]{2,1,0:T(2,128)(2,1)} %copy.126), calls=%async_computation.3 | async-start | bytes 6291456 | tf_op jit(solution)/shard_map/while/body/eval_jaxpr/all_to_all | solution.py:268
  317.1 309.3 %reduce-scatter.13.cloned.1.call-start = ((), (), s32[]{:S(2)}) async-start(), calls=%async_computation.14 | async-start | bytes 245760 | tf_op jit(solution)/shard_map/while/body/eval_jaxpr/reduce_scatter | solution.py:196
  321.8 380.5 %reduce-scatter.25.cloned.1.call-start = ((), (), s32[]{:S(2)}) async-start(), calls=%async_computation.22 | async-start | bytes 811008
  374.0 426.8 %reduce-scatter.21.cloned.1.call-start = ((), (), s32[]{:S(2)}) async-start(), calls=%async_computation.20 | async-start | bytes 5308416 | tf_op jit(solution)/shard_map/reduce_scatter | solution.py:338
  377.6 521.9 %reduce-scatter.23.cloned.1.call-start = ((), (), s32[]{:S(2)}) async-start(), calls=%async_computation.21 | async-start | bytes 5308416 | tf_op jit(solution)/shard_map/reduce_scatter | solution.py:341
  386.1 8.6 all-to-all-start.1
  542.2 36.6 %copy-start.40 = (f32[16]{0:T(128)S(1)}, f32[16]{0:T(128)}, u32[]{:S(2)}) copy-start(f32[16]{0:T(128)} %copy-done.39) | copy-start | bytes 196
  542.2 36.6 %copy-start.49 = (f32[16]{0:T(128)S(1)}, f32[16]{0:T(128)}, u32[]{:S(2)}) copy-start(f32[16]{0:T(128)} %copy-done.48) | copy-start | bytes 196
  548.5 34.2 %copy-start.32 = (f32[1536]{0:T(1024)S(1)}, f32[1536]{0:T(1024)}, u32[]{:S(2)}) copy-start(f32[1536]{0:T(1024)} %get-tuple-element.98) | copy-start | bytes 18436
  548.5 34.2 %copy-start.46 = (f32[1536]{0:T(1024)S(1)}, f32[1536]{0:T(1024)}, u32[]{:S(2)}) copy-start(f32[1536]{0:T(1024)} %get-tuple-element.87) | copy-start | bytes 18436
  548.5 34.2 %copy-start.47 = (f32[1536]{0:T(1024)S(1)}, f32[1536]{0:T(1024)}, u32[]{:S(2)}) copy-start(f32[1536]{0:T(1024)} %get-tuple-element.90) | copy-start | bytes 18436
  548.5 77.8 %copy-start.24 = (bf16[16,1536]{1,0:T(8,128)(2,1)S(1)}, bf16[16,1536]{1,0:T(8,128)(2,1)}, u32[]{:S(2)}) copy-start(bf16[16,1536]{1,0:T(8,128)(2,1)} %reduce-scatter.15.cloned.1.call-done) | copy-start | bytes 147460
  548.5 77.8 %copy-start.26 = (bf16[1,16,1536]{2,1,0:T(8,128)(2,1)S(1)}, bf16[1,16,1536]{2,1,0:T(8,128)(2,1)}, u32[]{:S(2)}) copy-start(bf16[1,16,1536]{2,1,0:T(8,128)(2,1)} %param.33) | copy-start | bytes 147460
  548.5 77.8 %copy-start.37 = (f32[16]{0:T(128)S(1)}, f32[16]{0:T(128)}, u32[]{:S(2)}) copy-start(f32[16]{0:T(128)} %copy-done.36) | copy-start | bytes 196
  548.5 77.8 %copy-start.42 = (f32[16]{0:T(128)S(1)}, f32[16]{0:T(128)}, u32[]{:S(2)}) copy-start(f32[16]{0:T(128)} %copy-done.41) | copy-start | bytes 196
  548.6 77.8 %copy-start.51 = (f32[16]{0:T(128)S(1)}, f32[16]{0:T(128)}, u32[]{:S(2)}) copy-start(f32[16]{0:T(128)} %copy-done.50) | copy-start | bytes 196
  548.6 77.8 %copy-start.53 = (f32[16]{0:T(128)S(1)}, f32[16]{0:T(128)}, u32[]{:S(2)}) copy-start(f32[16]{0:T(128)} %copy-done.52) | copy-start | bytes 196
  578.8 322.9 %copy-start.1 = (bf16[8,1536]{1,0:T(8,128)(2,1)S(1)}, bf16[8,1536]{1,0:T(8,128)(2,1)}, u32[]{:S(2)}) copy-start(bf16[8,1536]{1,0:T(8,128)(2,1)} %param.21) | copy-start | bytes 73732
  (35 other events, 156.6 us)
Sparse Core Ops, SparseCore 0:
  10.8 61.7 all-gather.8
  74.7 46.3 all-gather.6
  123.3 41.1 all-gather.10
  167.4 18.4 reduce-scatter.10
  207.8 19.7 reduce-scatter.14
  229.0 64.0 all-gather.12
  296.5 64.6 reduce-scatter.18
  365.2 63.7 reduce-scatter.16
  432.6 107.5 all-reduce.10
  542.3 36.5 all-gather.14
  581.3 19.8 reduce-scatter.12
  606.1 96.2 reduce-scatter.24
  706.0 94.7 reduce-scatter.20
  804.3 95.2 reduce-scatter.22
